TPU v7x, 512 devices: a whole 4x4x16 slice. The times are simulated.
512 devices in a mesh: dp: 16 (over x_hi, y, core), seq: 32 (over x_lo, z).
Axes of the slice: x: 4 (x_hi: 2, x_lo: 2; x = x_hi * 2 + x_lo), y: 4, z: 16, core: 2. Of those that a mesh axis runs over, the one named last changes fastest.
Arguments:
- queries: bfloat16 [16, 32768, 128], P('dp', 'seq'), may hold values from -6 to 6
- key_vectors: bfloat16 [16, 32768, 128], P('dp', 'seq'), may hold values from -6 to 6
- value_vectors: bfloat16 [16, 32768, 128], P('dp', 'seq'), may hold values from -6 to 6
- out_grad: bfloat16 [16, 32768, 128], P('dp', 'seq'), may hold values from -6 to 6
- log_decay: float32 [16, 1, 32768], P('dp', None, 'seq'), may hold values from -0.8 to 0, as said below
- prev_grads: bfloat16 [16, 1024, 6144], P('dp', 'seq'), may hold values from -6 to 6
Outputs:
- attn_out: bfloat16 [16, 32768, 128], P('dp', 'seq')
- grad_query: bfloat16 [16, 32768, 128], P('dp', 'seq')
- grad_key: bfloat16 [16, 32768, 128], P('dp', 'seq')
- grad_value: bfloat16 [16, 32768, 128], P('dp', 'seq')
- grad_shard: float32 [1024, 6144], P('seq', 'dp')
Inputs may be any that keep to these rules, and one draw needn't show every extreme that they name: `log_decay`: every entry is negative.
All inputs are finite; a program needn't handle non-finite values.
Results may differ from a plain program's by a relative error of at most 0.012.
Values may be sent and summed in bfloat16 or wider, within the bound.
A program may use at most 64 MiB of HBM per device.

v0:
```python
import jax
import jax.numpy as jnp
from jax import lax
from jax.sharding import PartitionSpec as P

BLK = 512
NORM_EPS = 1e-06
FULL_PRECISION = lax.Precision.HIGHEST


def product(left, right):
    return jnp.dot(left, right, precision=FULL_PRECISION, preferred_element_type=jnp.float32)


def decay_mask(running):
    spread = running[:, None] - running[None, :]
    lower_mask = jnp.tril(jnp.ones(spread.shape, dtype=bool))
    return jnp.where(lower_mask, jnp.exp(jnp.minimum(spread, 0.0)), 0.0)


def forward_local(query_head, key_head, value_head, decay_head):
    head_width = query_head.shape[-1]

    def advance(carried, block_inputs):
        query_block, key_block, value_block, decay_block = block_inputs
        running = jnp.cumsum(decay_block)
        scores = jnp.dot(query_block, key_block.T, preferred_element_type=jnp.float32) * decay_mask(
            running
        )
        query_wide = query_block.astype(jnp.float32)
        key_wide = key_block.astype(jnp.float32)
        value_wide = value_block.astype(jnp.float32)
        block_out = product(scores, value_wide) + jnp.exp(running)[:, None] * product(
            query_wide, carried
        )
        weights = jnp.exp(running[-1] - running)
        updated = jnp.exp(running[-1]) * carried + product(
            (key_wide * weights[:, None]).T, value_wide
        )
        return (updated, (block_out, carried))

    return lax.scan(
        advance,
        jnp.zeros((head_width, head_width), jnp.float32),
        (query_head, key_head, value_head, decay_head),
    )


def backward_local(query_head, key_head, value_head, dattn_head, decay_head, start_head):
    head_width = query_head.shape[-1]

    def retreat(later_sum, block_inputs):
        query_block, key_block, value_block, dattn_block, decay_block, carried = block_inputs
        running = jnp.cumsum(decay_block)
        decay_weights = decay_mask(running)
        scores = (
            jnp.dot(query_block, key_block.T, preferred_element_type=jnp.float32) * decay_weights
        )
        query_wide = query_block.astype(jnp.float32)
        key_wide = key_block.astype(jnp.float32)
        value_wide = value_block.astype(jnp.float32)
        dscores = product(dattn_block, value_wide.T) * decay_weights
        lead_decay = jnp.exp(running)[:, None]
        tail_decay = jnp.exp(running[-1] - running)[:, None]
        grad_q = product(dscores, key_wide) + lead_decay * product(dattn_block, carried.T)
        grad_k = product(dscores.T, query_wide) + tail_decay * product(value_wide, later_sum.T)
        grad_v = product(scores.T, dattn_block) + tail_decay * product(key_wide, later_sum)
        updated = jnp.exp(running[-1]) * later_sum + product(
            (query_wide * lead_decay).T, dattn_block
        )
        return (updated, (grad_q, grad_k, grad_v))

    return lax.scan(
        retreat,
        jnp.zeros((head_width, head_width), jnp.float32),
        (query_head, key_head, value_head, dattn_head, decay_head, start_head),
        reverse=True,
    )


def weigh_fold(block_logs, own_index, upward, running_sum, shard_part):
    summed_logs = jnp.cumsum(block_logs, axis=0)
    own_cum = lax.dynamic_index_in_dim(summed_logs, own_index, 0, keepdims=False)
    own_log = lax.dynamic_index_in_dim(block_logs, own_index, 0, keepdims=False)
    piece_count = shard_part.shape[0]
    token_offsets = jnp.arange(piece_count, dtype=jnp.int32)
    if upward:
        spread = summed_logs - block_logs - own_cum[None, :]
        usable = token_offsets > own_index
    else:
        spread = own_cum[None, :] - own_log[None, :] - summed_logs
        usable = token_offsets < own_index
    weights = jnp.where(usable[:, None], jnp.exp(jnp.minimum(spread, 0.0)), 0.0)
    return running_sum + jnp.einsum("nh,nhab->hab", weights, shard_part, precision=FULL_PRECISION)


def local(queries, key_vectors, value_vectors, out_grad, log_decay, prev_grads):
    row_count = queries.shape[1]
    head_count = log_decay.shape[1]
    head_width = queries.shape[2] // head_count
    block_count = row_count // BLK

    def by_head(tensor):
        return tensor[0].reshape(row_count, head_count, head_width).transpose(1, 0, 2)

    def by_block(tensor):
        return tensor.reshape(head_count, block_count, BLK, head_width)

    def to_rows(tensor):
        return (
            tensor.transpose(1, 0, 2)
            .reshape(1, row_count, head_count * head_width)
            .astype(jnp.bfloat16)
        )

    query_heads = by_head(queries)
    key_heads = by_head(key_vectors)
    value_heads = by_head(value_vectors)
    decay_rows = log_decay[0]
    decay_blocks = decay_rows.reshape(head_count, block_count, BLK)
    cumulative = jnp.cumsum(decay_rows, axis=1)
    log_total = cumulative[:, -1]
    local_state, (local_out, block_starts) = jax.vmap(forward_local)(
        by_block(query_heads), by_block(key_heads), by_block(value_heads), decay_blocks
    )
    identity = (
        jnp.zeros((head_count,), jnp.float32),
        jnp.zeros((head_count, head_width, head_width), jnp.float32),
    )
    own_index = lax.axis_index("seq")
    block_logs = lax.all_gather(log_total[None], "seq", axis=0, tiled=True)
    incoming = weigh_fold(
        block_logs,
        own_index,
        False,
        identity[1],
        lax.all_gather(local_state[None].astype(jnp.bfloat16), "seq", axis=0, tiled=True).astype(
            jnp.float32
        ),
    )
    query_wide = query_heads.astype(jnp.float32)
    key_wide = key_heads.astype(jnp.float32)
    value_wide = value_heads.astype(jnp.float32)
    lead_decay = jnp.exp(cumulative)[:, :, None]
    attention = local_out.reshape(head_count, row_count, head_width) + lead_decay * jnp.einsum(
        "hta,hab->htb", query_wide, incoming, precision=FULL_PRECISION
    )
    norm_ratio = lax.rsqrt(jnp.mean(attention * attention, axis=-1, keepdims=True) + NORM_EPS)
    attn_out = to_rows(attention * norm_ratio)
    cotangent = by_head(out_grad).astype(jnp.float32)
    cubed = norm_ratio * norm_ratio * norm_ratio
    dattn = (
        norm_ratio * cotangent
        - cubed / head_width * jnp.sum(cotangent * attention, axis=-1, keepdims=True) * attention
    )
    local_future, (grad_q_local, grad_k_local, grad_v_local) = jax.vmap(backward_local)(
        by_block(query_heads),
        by_block(key_heads),
        by_block(value_heads),
        by_block(dattn),
        decay_blocks,
        block_starts,
    )
    outgoing = weigh_fold(
        block_logs,
        own_index,
        True,
        identity[1],
        lax.all_gather(local_future[None].astype(jnp.bfloat16), "seq", axis=0, tiled=True).astype(
            jnp.float32
        ),
    )
    tail_decay = jnp.exp(log_total[:, None] - cumulative)[:, :, None]
    grad_query = grad_q_local.reshape(head_count, row_count, head_width) + lead_decay * jnp.einsum(
        "htb,hab->hta", dattn, incoming, precision=FULL_PRECISION
    )
    grad_key = grad_k_local.reshape(head_count, row_count, head_width) + tail_decay * jnp.einsum(
        "htb,hab->hta", value_wide, outgoing, precision=FULL_PRECISION
    )
    grad_value = grad_v_local.reshape(head_count, row_count, head_width) + tail_decay * jnp.einsum(
        "hta,hab->htb", key_wide, outgoing, precision=FULL_PRECISION
    )
    summed = lax.psum_scatter(
        prev_grads.astype(jnp.float32).astype(jnp.bfloat16), "dp", scatter_dimension=2, tiled=True
    ).astype(jnp.float32)
    return (attn_out, to_rows(grad_query), to_rows(grad_key), to_rows(grad_value), summed[0])


def solution(mesh):
    return jax.shard_map(
        local,
        mesh=mesh,
        in_specs=(
            P("dp", "seq", None),
            P("dp", "seq", None),
            P("dp", "seq", None),
            P("dp", "seq", None),
            P("dp", None, "seq"),
            P("dp", "seq", None),
        ),
        out_specs=(
            P("dp", "seq", None),
            P("dp", "seq", None),
            P("dp", "seq", None),
            P("dp", "seq", None),
            P("seq", "dp"),
        ),
        check_vma=False,
    )
```

profile of v0, /device:TPU:8, one launch (start us, length us, event | category | flops | bytes accessed | tf_op | source)
XLA Modules:
  0.0 324.7 jit_solution(16678804130265049411)
XLA Ops:
  8.1 15.7 %while.36 = (s32[]{:T(128)}, f32[1,128,128]{2,1,0:T(8,128)S(1)}, f32[2,1,512,128]{3,2,1,0:T(8,128)S(1)}, f32[2,1,128,128]{3,2,1,0:T(8,128)S(1)}, f32[2,1,512]{2,...) while((s32[]{:T(128)}, f32[1,128,128]{2,1,0:T(8,128)S(1)}, ...), condition=%wide.region_3.4_spmd.clone, body=%wide.region_0.3_spmd.clone.sunk | while | flops 672809472 | bytes 7176599 | solution.py:42
  8.2 0.8 constant_dynamic-slice_fusion.5
  9.2 0.6 slice.78
  10.2 0.6 slice.79
  12.3 1.3 convolution_multiply_fusion.14
  13.6 1.5 fusion.176
  15.4 0.5 fusion.175
  16.0 0.8 constant_dynamic-slice_fusion.5
  17.1 0.6 slice.78
  18.1 0.6 slice.79
  20.1 1.3 convolution_multiply_fusion.14
  21.4 1.5 fusion.176
  23.2 0.5 fusion.175
  23.8 0.7 convert_element_type.117
  24.6 6.1 %copy.49 = bf16[1,32,6144]{1,0,2:T(2,128)(2,1)S(1)} copy(bf16[1,32,6144]{2,1,0:T(8,128)(2,1)} %param.15) | data formatting | bytes 786432
  30.7 1.4 copy.57
  32.7 0.6 slice.60
  33.5 0.6 slice.61
  34.1 1.3 dynamic-slice
  36.7 0.7 bitcast_dynamic-update-slice_fusion.1
  37.4 70.7 %all-reduce = f32[32]{0:T(128)S(1)} all-reduce(f32[32]{0:T(128)S(1)} %bitcast_dynamic-update-slice_fusion.1), channel_id=1, replica_groups=mesh['dp'=16,'seq'=32] {'seq'}, use_global_device_ids=true, to_apply=%add | all-reduce | flops 32 | bytes 256
  108.1 0.6 dynamic-slice.1
  108.8 1.1 copy.33
  109.9 1.2 copy.45
  111.2 1.2 fusion.120
  112.4 2.0 select_reduce_fusion
  114.4 46.8 %all-gather.5.cloned.1.call-done = bf16[32,128,128]{2,1,0:T(8,128)(2,1)} async-done(((bf16[1,128,128]{2,1,0:T(8,128)(2,1)}), bf16[32,128,128]{2,1,0:T(8,128)(2,1)}) %all-gather.5.cloned.1.call-update) | async-done | bytes 1048592 | tf_op jit(solution)/shard_map/all_gather | solution.py:137
  161.2 2.2 fusion.105
  163.4 0.5 fusion.108
  164.4 0.8 broadcast.304
  165.2 21.6 %while.37 = (s32[]{:T(128)}, f32[1,128,128]{2,1,0:T(8,128)S(1)}, f32[2,1,512,128]{3,2,1,0:T(8,128)}, f32[2,1,512,128]{3,2,1,0:T(8,128)S(1)}, f32[2,1,512,128]{3,...) while((s32[]{:T(128)}, f32[1,128,128]{2,1,0:T(8,128)S(1)}, ...), condition=%wide.region_12.13_spmd.clone, body=%wide.region_9.12_spmd.clone.sunk | while | flops 2083668480 | bytes 14791102 | solution.py:73
  165.5 0.6 slice.82
  166.3 0.7 reduce-window.55
  167.0 0.7 slice_bitcast_fusion.6
  167.8 0.6 slice.83
  169.8 0.6 convolution_multiply_fusion.15
  170.4 1.0 fusion.199
  171.5 0.6 fusion.197
  172.1 0.4 fusion.198
  172.8 0.3 convolution_multiply_fusion.16
  173.1 1.8 fusion.201
  175.3 0.7 fusion.196
  176.3 0.6 slice.82
  177.1 0.7 reduce-window.55
  177.8 0.7 slice_bitcast_fusion.6
  178.6 0.6 slice.83
  180.6 0.7 convolution_multiply_fusion.15
  181.2 1.0 fusion.199
  182.3 0.6 fusion.197
  182.9 0.4 fusion.198
  183.9 1.8 fusion.201
  186.1 0.7 fusion.196
  186.8 0.6 convert_element_type.124
  187.5 1.0 reshape_bitcast_fusion
  188.6 0.6 bitcast_convert_fusion
  189.2 0.7 fusion.110
  190.0 0.8 copy.38
  191.2 1.7 fusion.102
  193.0 119.5 %all-gather.7.cloned.1.call-done = bf16[32,128,128]{2,1,0:T(8,128)(2,1)} async-done(((bf16[1,128,128]{2,1,0:T(8,128)(2,1)}), bf16[32,128,128]{2,1,0:T(8,128)(2,1)}) %all-gather.7.cloned.1.call-update) | async-done | bytes 1048592 | tf_op jit(solution)/shard_map/all_gather | solution.py:169
  312.5 2.2 fusion.103
  314.7 0.4 fusion.100
  315.2 0.8 copy.40
  316.0 0.4 fusion.101
  316.4 0.8 copy.39
  (110 shorter events, 7.2 us)
Async XLA Ops:
  8.0 153.2 %all-gather.5.cloned.1.call-start = ((), (), s32[]{:S(2)}) async-start(), calls=%async_computation.1 | async-start | bytes 1081344 | tf_op jit(solution)/shard_map/all_gather | solution.py:137
  8.1 7.0 %copy-start.4 = (bf16[2,1,512,128]{3,2,1,0:T(8,128)(2,1)S(1)}, bf16[2,1,512,128]{3,2,1,0:T(8,128)(2,1)}, u32[]{:S(2)}) copy-start(bf16[2,1,512,128]{3,2,1,0:T(8,128)(2,1)} %get-tuple-element.592) | copy-start | bytes 786436 | tf_op jit(solution)/shard_map/vmap()/while
  8.1 7.2 %copy-start = (bf16[2,1,512,128]{3,2,1,0:T(8,128)(2,1)S(1)}, bf16[2,1,512,128]{3,2,1,0:T(8,128)(2,1)}, u32[]{:S(2)}) copy-start(bf16[2,1,512,128]{3,2,1,0:T(8,128)(2,1)} %get-tuple-element.590) | copy-start | bytes 786436 | tf_op jit(solution)/shard_map/vmap()/while
  8.1 7.2 %copy-start.2 = (bf16[2,1,512,128]{3,2,1,0:T(8,128)(2,1)S(1)}, bf16[2,1,512,128]{3,2,1,0:T(8,128)(2,1)}, u32[]{:S(2)}) copy-start(bf16[2,1,512,128]{3,2,1,0:T(8,128)(2,1)} %get-tuple-element.591) | copy-start | bytes 786436 | tf_op jit(solution)/shard_map/vmap()/while
  16.0 7.0 %copy-start.4 = (bf16[2,1,512,128]{3,2,1,0:T(8,128)(2,1)S(1)}, bf16[2,1,512,128]{3,2,1,0:T(8,128)(2,1)}, u32[]{:S(2)}) copy-start(bf16[2,1,512,128]{3,2,1,0:T(8,128)(2,1)} %get-tuple-element.592) | copy-start | bytes 786436 | tf_op jit(solution)/shard_map/vmap()/while
  16.0 7.3 %copy-start = (bf16[2,1,512,128]{3,2,1,0:T(8,128)(2,1)S(1)}, bf16[2,1,512,128]{3,2,1,0:T(8,128)(2,1)}, u32[]{:S(2)}) copy-start(bf16[2,1,512,128]{3,2,1,0:T(8,128)(2,1)} %get-tuple-element.590) | copy-start | bytes 786436 | tf_op jit(solution)/shard_map/vmap()/while
  16.0 7.2 %copy-start.2 = (bf16[2,1,512,128]{3,2,1,0:T(8,128)(2,1)S(1)}, bf16[2,1,512,128]{3,2,1,0:T(8,128)(2,1)}, u32[]{:S(2)}) copy-start(bf16[2,1,512,128]{3,2,1,0:T(8,128)(2,1)} %get-tuple-element.591) | copy-start | bytes 786436 | tf_op jit(solution)/shard_map/vmap()/while
  23.8 0.8 copy-start.9
  23.8 6.9 %copy-start.10 = (f32[2,1,128,128]{3,2,1,0:T(8,128)}, f32[2,1,128,128]{3,2,1,0:T(8,128)S(1)}, u32[]{:S(2)}) copy-start(f32[2,1,128,128]{3,2,1,0:T(8,128)S(1)} %get-tuple-element.606) | copy-start | bytes 393220
  24.6 162.9 %reduce-scatter.4.cloned.1.call-start = ((), (), s32[]{:S(2)}) async-start(), calls=%async_computation.3 | async-start | bytes 1671168
  30.7 1.5 copy-start.12
  32.1 131.3 %copy-start.5 = (bf16[2,1,512,128]{3,2,1,0:T(8,128)(2,1)S(1)}, bf16[2,1,512,128]{3,2,1,0:T(8,128)(2,1)}, u32[]{:S(2)}) copy-start(bf16[2,1,512,128]{3,2,1,0:T(8,128)(2,1)} %get-tuple-element.645) | copy-start | bytes 786436
  32.1 280.4 %all-gather.7.cloned.1.call-start = ((), (), s32[]{:S(2)}) async-start(), calls=%async_computation.2 | async-start | bytes 1081344 | tf_op jit(solution)/shard_map/all_gather | solution.py:169
  108.1 55.9 %copy-start.13 = (f32[1024]{0:T(1024)}, f32[1024]{0:T(1024)S(1)}, u32[]{:S(2)}) copy-start(f32[1024]{0:T(1024)S(1)} %get-tuple-element.432) | copy-start | bytes 12292
  163.3 1.9 copy-start.1
  163.4 1.8 copy-start.3
  163.9 1.3 copy-start.15
  167.0 5.1 %copy-start.6 = (f32[2,1,512,128]{3,2,1,0:T(8,128)S(1)}, f32[2,1,512,128]{3,2,1,0:T(8,128)}, u32[]{:S(2)}) copy-start(f32[2,1,512,128]{3,2,1,0:T(8,128)} %get-tuple-element.612) | copy-start | bytes 1572868 | tf_op jit(solution)/shard_map/vmap()/while
  167.0 5.1 %copy-start.11 = (f32[2,1,128,128]{3,2,1,0:T(8,128)S(1)}, f32[2,1,128,128]{3,2,1,0:T(8,128)}, u32[]{:S(2)}) copy-start(f32[2,1,128,128]{3,2,1,0:T(8,128)} %get-tuple-element.634) | copy-start | bytes 393220 | tf_op jit(solution)/shard_map/vmap()/while
  172.5 3.5 %copy-start.7 = (f32[2,1,512,128]{3,2,1,0:T(8,128)}, f32[2,1,512,128]{3,2,1,0:T(8,128)S(1)}, u32[]{:S(2)}) copy-start(f32[2,1,512,128]{3,2,1,0:T(8,128)S(1)} %fusion.198) | copy-start | bytes 1572868 | tf_op jit(solution)/shard_map/vmap()/while
  177.8 5.1 %copy-start.6 = (f32[2,1,512,128]{3,2,1,0:T(8,128)S(1)}, f32[2,1,512,128]{3,2,1,0:T(8,128)}, u32[]{:S(2)}) copy-start(f32[2,1,512,128]{3,2,1,0:T(8,128)} %get-tuple-element.612) | copy-start | bytes 1572868 | tf_op jit(solution)/shard_map/vmap()/while
  177.8 5.1 %copy-start.11 = (f32[2,1,128,128]{3,2,1,0:T(8,128)S(1)}, f32[2,1,128,128]{3,2,1,0:T(8,128)}, u32[]{:S(2)}) copy-start(f32[2,1,128,128]{3,2,1,0:T(8,128)} %get-tuple-element.634) | copy-start | bytes 393220 | tf_op jit(solution)/shard_map/vmap()/while
  183.3 3.5 %copy-start.7 = (f32[2,1,512,128]{3,2,1,0:T(8,128)}, f32[2,1,512,128]{3,2,1,0:T(8,128)S(1)}, u32[]{:S(2)}) copy-start(f32[2,1,512,128]{3,2,1,0:T(8,128)S(1)} %fusion.198) | copy-start | bytes 1572868 | tf_op jit(solution)/shard_map/vmap()/while
  186.8 4.4 %copy-start.8 = (f32[2,1,512,128]{3,2,1,0:T(8,128)S(1)}, f32[2,1,512,128]{3,2,1,0:T(8,128)}, u32[]{:S(2)}) copy-start(f32[2,1,512,128]{3,2,1,0:T(8,128)} %get-tuple-element.272) | copy-start | bytes 1572868
  186.8 4.4 %copy-start.14 = (f32[1024]{0:T(1024)S(1)}, f32[1024]{0:T(1024)}, u32[]{:S(2)}) copy-start(f32[1024]{0:T(1024)} %copy-done.13) | copy-start | bytes 12292
  186.8 125.7 %copy-start.16 = (f32[32]{0:T(128)S(1)}, f32[32]{0:T(128)}, u32[]{:S(2)}) copy-start(f32[32]{0:T(128)} %get-tuple-element.387) | copy-start | bytes 388
Sparse Core Ops, SparseCore 0:
  24.6 136.4 all-gather.4
  187.6 124.8 all-gather.6
Sparse Core Ops, SparseCore 1:
  32.2 96.2 reduce-scatter.3
where the time goes:
time: 326 us; the launch traced here: 325 us
  waiting for transfers between devices  166 us (51%)
  blocking collectives  70.7 us (22%)
  local copies, waits for them, and re-layouts  27.9 us (9%)
  matrix products  26.8 us (8%)
  between operations  17.1 us (5%)
  other arithmetic  9.85 us (3%)
  loops' own time  5.81 us (2%)
    all_gather x1, waiting for transfers between devices, local(): lax.all_gather(local_future[None].astype(jnp.bfloat16), 'seq', axis=0, ti...  120 us
    unnamed x1, blocking collectives  70.7 us
    all_gather x1, waiting for transfers between devices, local(): lax.all_gather(local_state[None].astype(jnp.bfloat16), 'seq', axis=0, til...  46.8 us
    dot_general x22, matrix products, product(): jnp.dot(left, right, precision=FULL_PRECISION, preferred_element_type=jnp...  16.3 us
    unnamed x36, local copies, waits for them, and re-layouts  15.1 us
  transfers between devices with their start and end apart: 3, of which 2 were waited for; matrix products, arithmetic and copies ran while one was open for 14% of the time, Pallas kernels for 0%

commit v1 on v0

--- a/solution.py
+++ b/solution.py
@@ -129,14 +129,18 @@
     )
     own_index = lax.axis_index("seq")
     block_logs = lax.all_gather(log_total[None], "seq", axis=0, tiled=True)
+    turns_raise = lambda arr, link_axis: jnp.concatenate(
+        jax.lax.all_to_all(
+            jnp.stack([arr for _ in range(jax.lax.axis_size(link_axis))], axis=0), link_axis, 0, 0
+        ),
+        axis=0,
+    )
     incoming = weigh_fold(
         block_logs,
         own_index,
         False,
         identity[1],
-        lax.all_gather(local_state[None].astype(jnp.bfloat16), "seq", axis=0, tiled=True).astype(
-            jnp.float32
-        ),
+        turns_raise(local_state[None].astype(jnp.bfloat16), "seq").astype(jnp.float32),
     )
     query_wide = query_heads.astype(jnp.float32)
     key_wide = key_heads.astype(jnp.float32)

time: 326 us -> 315 us (0.966)
  waiting for transfers between devices: 166 us -> 120 us
  blocking collectives: 70.7 us -> 89.6 us
  starting transfers between devices: 0.08 us -> 16.6 us
    all_gather x1 -> x0, waiting for transfers between devices: 46.8 us -> none  [local(): lax.all_gather(local_state[None].astype(jnp.bfloat16), 'seq', axis=0, til...]
    unnamed x1, blocking collectives: 70.7 us -> 89.6 us
    all_to_all x0 -> x1, starting transfers between devices: none -> 16.5 us  [local(): jax.lax.all_to_all(jnp.stack([arr for _ in range(jax.lax.axis_size(link_a...]
    unnamed x36 -> x38, local copies, waits for them, and re-layouts: 15.1 us -> 14.1 us
  transfers between devices with their start and end apart: 3 -> 3, of which waited for: 2 -> 1; matrix products, arithmetic and copies ran while one was open for 14% -> 15% of each run, Pallas kernels for 0% -> 0%
where the time goes in v1:
time: 315 us; the launch traced here: 314 us
  waiting for transfers between devices  120 us (38%)
  blocking collectives  89.6 us (28%)
  local copies, waits for them, and re-layouts  28.3 us (9%)
  matrix products  26.9 us (9%)
  between operations  17.1 us (5%)
  starting transfers between devices  16.6 us (5%)
  other arithmetic  9.27 us (3%)
  loops' own time  5.89 us (2%)
    all_gather x1, waiting for transfers between devices, local(): lax.all_gather(local_future[None].astype(jnp.bfloat16), 'seq', axis=0, ti...  120 us
    unnamed x1, blocking collectives  89.6 us
    all_to_all x1, starting transfers between devices, local(): jax.lax.all_to_all(jnp.stack([arr for _ in range(jax.lax.axis_size(link_a...  16.5 us
    dot_general x22, matrix products, product(): jnp.dot(left, right, precision=FULL_PRECISION, preferred_element_type=jnp...  16.3 us
    unnamed x38, local copies, waits for them, and re-layouts  14.1 us
  transfers between devices with their start and end apart: 3, of which 1 were waited for; matrix products, arithmetic and copies ran while one was open for 15% of the time, Pallas kernels for 0%

profile of v1, /device:TPU:8, one launch (start us, length us, event | category | flops | bytes accessed | tf_op | source)
XLA Modules:
  0.0 313.6 jit_solution(13078067399122757379)
XLA Ops:
  8.1 15.7 %while.36 = (s32[]{:T(128)}, f32[1,128,128]{2,1,0:T(8,128)S(1)}, f32[2,1,512,128]{3,2,1,0:T(8,128)S(1)}, f32[2,1,128,128]{3,2,1,0:T(8,128)S(1)}, f32[2,1,512]{2,...) while((s32[]{:T(128)}, f32[1,128,128]{2,1,0:T(8,128)S(1)}, ...), condition=%wide.region_3.4_spmd.clone, body=%wide.region_0.3_spmd.clone.sunk | while | flops 672809472 | bytes 7176599 | solution.py:42
  8.1 0.8 constant_dynamic-slice_fusion.5
  9.2 0.6 slice.78
  10.2 0.6 slice.79
  12.2 1.3 convolution_multiply_fusion.14
  13.5 1.5 fusion.176
  15.3 0.5 fusion.175
  15.9 0.8 constant_dynamic-slice_fusion.5
  17.0 0.6 slice.78
  18.0 0.6 slice.79
  20.1 1.3 convolution_multiply_fusion.14
  21.3 1.5 fusion.176
  23.2 0.5 fusion.175
  23.8 1.2 stack.2
  25.0 16.5 %all-to-all-start = ((bf16[32,1,1,128,128]{4,3,2,1,0:T(8,128)(2,1)}), bf16[32,1,1,128,128]{4,3,2,1,0:T(8,128)(2,1)}, u32[]{:S(2)}, u32[]{:S(2)}) async-start(bf16[32,1,1,128,128]{4,3,2,1,0:T(8,128)(2,1)} %stack.2), calls=%async_computation | async-start | bytes 2097152 | tf_op jit(solution)/shard_map/all_to_all | solution.py:133
  41.6 6.1 %copy.49 = bf16[1,32,6144]{1,0,2:T(2,128)(2,1)S(1)} copy(bf16[1,32,6144]{2,1,0:T(8,128)(2,1)} %param.15) | data formatting | bytes 786432
  47.8 1.4 copy.57
  49.5 0.6 slice.60
  50.5 0.6 slice.61
  51.1 1.3 dynamic-slice
  53.7 0.7 bitcast_dynamic-update-slice_fusion.1
  54.4 89.6 %all-reduce = f32[32]{0:T(128)S(1)} all-reduce(f32[32]{0:T(128)S(1)} %bitcast_dynamic-update-slice_fusion.1), channel_id=1, replica_groups=mesh['dp'=16,'seq'=32] {'seq'}, use_global_device_ids=true, to_apply=%add | all-reduce | flops 32 | bytes 256
  144.0 0.6 dynamic-slice.1
  144.9 1.2 copy.45
  146.2 1.2 fusion.120
  147.3 1.9 select_reduce_fusion
  149.3 2.2 fusion.105
  151.6 0.5 fusion.108
  152.5 0.8 broadcast.306
  153.4 22.1 %while.37 = (s32[]{:T(128)}, f32[1,128,128]{2,1,0:T(8,128)S(1)}, f32[2,1,512,128]{3,2,1,0:T(8,128)}, f32[2,1,512,128]{3,2,1,0:T(8,128)S(1)}, f32[2,1,512,128]{3,...) while((s32[]{:T(128)}, f32[1,128,128]{2,1,0:T(8,128)S(1)}, ...), condition=%wide.region_12.13_spmd.clone, body=%wide.region_9.12_spmd.clone.sunk | while | flops 2083668480 | bytes 14791102 | solution.py:73
  153.7 0.6 slice.82
  154.5 0.8 reduce-window.55
  155.3 0.7 slice_bitcast_fusion.6
  156.1 0.7 slice.83
  158.2 0.7 convolution_multiply_fusion.15
  158.9 1.0 fusion.199
  159.9 0.6 fusion.197
  160.5 0.4 fusion.198
  161.2 0.3 convolution_multiply_fusion.16
  161.6 1.8 fusion.201
  163.7 0.7 fusion.196
  164.8 0.6 slice.82
  165.5 0.8 reduce-window.55
  166.3 0.7 slice_bitcast_fusion.6
  167.1 0.7 slice.83
  169.2 0.7 convolution_multiply_fusion.15
  169.9 1.0 fusion.199
  170.9 0.6 fusion.197
  171.5 0.4 fusion.198
  172.3 0.3 convolution_multiply_fusion.16
  172.6 1.8 fusion.201
  174.7 0.7 fusion.196
  175.5 0.6 convert_element_type.123
  176.2 1.0 reshape_bitcast_fusion
  177.3 0.6 bitcast_convert_fusion
  177.9 0.7 fusion.110
  178.6 0.8 copy.38
  179.9 1.7 fusion.102
  181.6 119.8 %all-gather.3.cloned.1.call-done = bf16[32,128,128]{2,1,0:T(8,128)(2,1)} async-done(((bf16[1,128,128]{2,1,0:T(8,128)(2,1)}), bf16[32,128,128]{2,1,0:T(8,128)(2,1)}) %all-gather.3.cloned.1.call-update) | async-done | bytes 1048592 | tf_op jit(solution)/shard_map/all_gather | solution.py:173
  301.5 2.2 fusion.103
  303.6 0.4 fusion.100
  304.1 0.8 copy.40
  304.9 0.4 fusion.101
  305.3 0.8 copy.39
  (112 shorter events, 7.0 us)
Async XLA Ops:
  8.1 7.0 %copy-start.4 = (bf16[2,1,512,128]{3,2,1,0:T(8,128)(2,1)S(1)}, bf16[2,1,512,128]{3,2,1,0:T(8,128)(2,1)}, u32[]{:S(2)}) copy-start(bf16[2,1,512,128]{3,2,1,0:T(8,128)(2,1)} %get-tuple-element.592) | copy-start | bytes 786436 | tf_op jit(solution)/shard_map/vmap()/while
  8.1 7.2 %copy-start = (bf16[2,1,512,128]{3,2,1,0:T(8,128)(2,1)S(1)}, bf16[2,1,512,128]{3,2,1,0:T(8,128)(2,1)}, u32[]{:S(2)}) copy-start(bf16[2,1,512,128]{3,2,1,0:T(8,128)(2,1)} %get-tuple-element.590) | copy-start | bytes 786436 | tf_op jit(solution)/shard_map/vmap()/while
  8.1 7.2 %copy-start.2 = (bf16[2,1,512,128]{3,2,1,0:T(8,128)(2,1)S(1)}, bf16[2,1,512,128]{3,2,1,0:T(8,128)(2,1)}, u32[]{:S(2)}) copy-start(bf16[2,1,512,128]{3,2,1,0:T(8,128)(2,1)} %get-tuple-element.591) | copy-start | bytes 786436 | tf_op jit(solution)/shard_map/vmap()/while
  15.9 7.0 %copy-start.4 = (bf16[2,1,512,128]{3,2,1,0:T(8,128)(2,1)S(1)}, bf16[2,1,512,128]{3,2,1,0:T(8,128)(2,1)}, u32[]{:S(2)}) copy-start(bf16[2,1,512,128]{3,2,1,0:T(8,128)(2,1)} %get-tuple-element.592) | copy-start | bytes 786436 | tf_op jit(solution)/shard_map/vmap()/while
  15.9 7.2 %copy-start = (bf16[2,1,512,128]{3,2,1,0:T(8,128)(2,1)S(1)}, bf16[2,1,512,128]{3,2,1,0:T(8,128)(2,1)}, u32[]{:S(2)}) copy-start(bf16[2,1,512,128]{3,2,1,0:T(8,128)(2,1)} %get-tuple-element.590) | copy-start | bytes 786436 | tf_op jit(solution)/shard_map/vmap()/while
  15.9 7.2 %copy-start.2 = (bf16[2,1,512,128]{3,2,1,0:T(8,128)(2,1)S(1)}, bf16[2,1,512,128]{3,2,1,0:T(8,128)(2,1)}, u32[]{:S(2)}) copy-start(bf16[2,1,512,128]{3,2,1,0:T(8,128)(2,1)} %get-tuple-element.591) | copy-start | bytes 786436 | tf_op jit(solution)/shard_map/vmap()/while
  23.7 17.8 %copy-start.9 = (f32[2,1,512,128]{3,2,1,0:T(8,128)}, f32[2,1,512,128]{3,2,1,0:T(8,128)S(1)}, u32[]{:S(2)}) copy-start(f32[2,1,512,128]{3,2,1,0:T(8,128)S(1)} %get-tuple-element.269) | copy-start | bytes 1572868
  23.7 17.8 %copy-start.10 = (f32[2,1,128,128]{3,2,1,0:T(8,128)}, f32[2,1,128,128]{3,2,1,0:T(8,128)S(1)}, u32[]{:S(2)}) copy-start(f32[2,1,128,128]{3,2,1,0:T(8,128)S(1)} %get-tuple-element.606) | copy-start | bytes 393220
  25.0 124.3 %all-to-all-start = ((bf16[32,1,1,128,128]{4,3,2,1,0:T(8,128)(2,1)}), bf16[32,1,1,128,128]{4,3,2,1,0:T(8,128)(2,1)}, u32[]{:S(2)}, u32[]{:S(2)}) async-start(bf16[32,1,1,128,128]{4,3,2,1,0:T(8,128)(2,1)} %stack.2), calls=%async_computation | async-start | bytes 2097152 | tf_op jit(solution)/shard_map/all_to_all | solution.py:133
  41.6 134.6 %reduce-scatter.4.cloned.1.call-start = ((), (), s32[]{:S(2)}) async-start(), calls=%async_computation.3 | async-start | bytes 1671168
  47.7 1.5 copy-start.13
  47.7 97.0 %copy-start.12 = (bf16[1,1024,128]{2,1,0:T(8,128)(2,1)S(1)}, bf16[1,1024,128]{2,1,0:T(8,128)(2,1)}, u32[]{:S(2)}) copy-start(bf16[1,1024,128]{2,1,0:T(8,128)(2,1)} %param.13) | copy-start | bytes 786436
  49.1 102.4 %copy-start.5 = (bf16[2,1,512,128]{3,2,1,0:T(8,128)(2,1)S(1)}, bf16[2,1,512,128]{3,2,1,0:T(8,128)(2,1)}, u32[]{:S(2)}) copy-start(bf16[2,1,512,128]{3,2,1,0:T(8,128)(2,1)} %get-tuple-element.644) | copy-start | bytes 786436
  49.1 252.3 %all-gather.3.cloned.1.call-start = ((), (), s32[]{:S(2)}) async-start(), calls=%async_computation.2 | async-start | bytes 1081344 | tf_op jit(solution)/shard_map/all_gather | solution.py:173
  149.3 3.2 %copy-start.14 = (f32[1024]{0:T(1024)}, f32[1024]{0:T(1024)S(1)}, u32[]{:S(2)}) copy-start(f32[1024]{0:T(1024)S(1)} %get-tuple-element.432) | copy-start | bytes 12292
  151.5 1.9 copy-start.1
  151.5 1.8 copy-start.3
  152.1 1.3 copy-start.16
  155.3 5.2 %copy-start.6 = (f32[2,1,512,128]{3,2,1,0:T(8,128)S(1)}, f32[2,1,512,128]{3,2,1,0:T(8,128)}, u32[]{:S(2)}) copy-start(f32[2,1,512,128]{3,2,1,0:T(8,128)} %get-tuple-element.612) | copy-start | bytes 1572868 | tf_op jit(solution)/shard_map/vmap()/while
  155.3 5.3 %copy-start.11 = (f32[2,1,128,128]{3,2,1,0:T(8,128)S(1)}, f32[2,1,128,128]{3,2,1,0:T(8,128)}, u32[]{:S(2)}) copy-start(f32[2,1,128,128]{3,2,1,0:T(8,128)} %get-tuple-element.634) | copy-start | bytes 393220 | tf_op jit(solution)/shard_map/vmap()/while
  160.9 3.5 %copy-start.7 = (f32[2,1,512,128]{3,2,1,0:T(8,128)}, f32[2,1,512,128]{3,2,1,0:T(8,128)S(1)}, u32[]{:S(2)}) copy-start(f32[2,1,512,128]{3,2,1,0:T(8,128)S(1)} %fusion.198) | copy-start | bytes 1572868 | tf_op jit(solution)/shard_map/vmap()/while
  166.3 5.2 %copy-start.6 = (f32[2,1,512,128]{3,2,1,0:T(8,128)S(1)}, f32[2,1,512,128]{3,2,1,0:T(8,128)}, u32[]{:S(2)}) copy-start(f32[2,1,512,128]{3,2,1,0:T(8,128)} %get-tuple-element.612) | copy-start | bytes 1572868 | tf_op jit(solution)/shard_map/vmap()/while
  166.3 5.3 %copy-start.11 = (f32[2,1,128,128]{3,2,1,0:T(8,128)S(1)}, f32[2,1,128,128]{3,2,1,0:T(8,128)}, u32[]{:S(2)}) copy-start(f32[2,1,128,128]{3,2,1,0:T(8,128)} %get-tuple-element.634) | copy-start | bytes 393220 | tf_op jit(solution)/shard_map/vmap()/while
  172.0 3.5 %copy-start.7 = (f32[2,1,512,128]{3,2,1,0:T(8,128)}, f32[2,1,512,128]{3,2,1,0:T(8,128)S(1)}, u32[]{:S(2)}) copy-start(f32[2,1,512,128]{3,2,1,0:T(8,128)S(1)} %fusion.198) | copy-start | bytes 1572868 | tf_op jit(solution)/shard_map/vmap()/while
  175.5 4.4 %copy-start.8 = (f32[2,1,512,128]{3,2,1,0:T(8,128)S(1)}, f32[2,1,512,128]{3,2,1,0:T(8,128)}, u32[]{:S(2)}) copy-start(f32[2,1,512,128]{3,2,1,0:T(8,128)} %get-tuple-element.272) | copy-start | bytes 1572868
  175.5 4.4 %copy-start.15 = (f32[1024]{0:T(1024)S(1)}, f32[1024]{0:T(1024)}, u32[]{:S(2)}) copy-start(f32[1024]{0:T(1024)} %copy-done.14) | copy-start | bytes 12292
  175.5 126.0 %copy-start.17 = (f32[32]{0:T(128)S(1)}, f32[32]{0:T(128)}, u32[]{:S(2)}) copy-start(f32[32]{0:T(128)} %get-tuple-element.387) | copy-start | bytes 388
Sparse Core Ops, SparseCore 0:
  49.3 92.4 reduce-scatter.3
Sparse Core Ops, SparseCore 1:
  176.2 125.2 all-gather.2
